TPU v7x, 256 devices: a whole 4x4x8 slice. The times are simulated.
256 devices in a mesh: sec: 2 (over y_lo), grp: 16 (over z, y_hi), tp: 8 (over x, core).
Axes of the slice: x: 4, y: 4 (y_hi: 2, y_lo: 2; y = y_hi * 2 + y_lo), z: 8, core: 2. Of those that a mesh axis runs over, the one named last changes fastest.
Arguments:
- hidden_in: bfloat16 [1024, 7168], P(('sec', 'grp', 'tp')), may hold values from -6 to 6
- queries: bfloat16 [1024, 16, 8, 576], P(('sec', 'grp'), None, 'tp'), may hold values from -61 to 61
- latent_cache: bfloat16 [1024, 64, 576], P(('sec', 'grp')), may hold values from -6 to 6
- lengths: int32 [1024], P(('sec', 'grp')), may hold values from 2 to 64, as said below
- w_uv: bfloat16 [16, 8, 512, 128], P(None, 'tp'), may hold values from -0.75 to 0.75
- attn_weight: bfloat16 [16, 8, 128, 7168], P(None, 'tp', None, 'grp'), may hold values from -0.125 to 0.125
- norm_gain: float32 [7168], replicated, may hold values from 0.1 to 1.9
- router: bfloat16 [7168, 32], replicated, may hold values from -0.0625 to 0.0625
- routes: int32 [1024, 8], P(('sec', 'grp', 'tp')), may hold values from 0 to 31, all different within a row; in each aligned block of 4 rows (0 to 3, 4 to 7, ...) at most 2 rows name the same one
- live_counts: int32 [256], P(('sec', 'grp', 'tp')), may hold values from 3 to 4, as said below
- expert_in: bfloat16 [32, 7168, 2, 1024], P(('sec', 'grp'), None, None, 'tp'), may hold values from -0.0625 to 0.0625
- expert_out: bfloat16 [32, 1024, 7168], P(('sec', 'grp'), 'tp'), may hold values from -0.5 to 0.5
Outputs:
- layer_out: bfloat16 [1024, 7168], P(('sec', 'grp', 'tp'))
Inputs may be any that keep to these rules, and one draw needn't show every extreme that they name: `lengths`: some request has exactly 64 cached positions and some has 2. `live_counts`: some device has all 4 slots live and some has exactly 3. `routes`: the 8 experts of a token differ. Within the rows of one device (aligned blocks of 4 rows) no expert is named by more than 2 rows, a bound that some block reaches.
All inputs are finite; a program needn't handle non-finite values.
Results may differ from a plain program's by a relative error of at most 0.018.
Values may be sent and summed in bfloat16 or wider, within the bound.
No kernel may reach another device: no remote copies, remote signals or barrier semaphores. Data moves between devices by JAX's collectives and lax.ppermute only.
A program may use at most 64 MiB of HBM per device.

v0:
```python
import jax
import jax.numpy as jnp
from jax import lax
from jax.sharding import Mesh
from jax.sharding import PartitionSpec as P

GRP = ("grp_0", "grp_1")
SEC_GRP = ("sec", "grp_0", "grp_1")
GRP_SEC = ("grp_0", "grp_1", "sec")
SEC_GRP_TP = ("sec", "grp_0", "grp_1", "tp")
score_scale = 192.0 ** (-0.5)
route_scale = 2.5


def gathered_by_axis(x, axes, dim):
    out = x
    for number in range(len(axes) - 1, -1, -1):
        out = lax.all_gather(out, axes[number], axis=dim, tiled=True)
    return out


def in_blocks(x, dim, peers):
    lengths = x.shape
    tiles = x.reshape(*lengths[:dim], peers, lengths[dim] // peers, *lengths[dim + 1 :])
    return jnp.moveaxis(tiles, dim, 0)


def sent_and_summed(x, axis, dim):
    tiles = in_blocks(x, dim, lax.axis_size(axis))
    arrived = lax.all_to_all(tiles, axis, split_axis=0, concat_axis=0, tiled=True)
    return arrived.astype(jnp.float32).sum(axis=0)


def in_order(tiles, dim):
    tiles = jnp.moveaxis(tiles, 0, dim)
    lengths = tiles.shape
    return tiles.reshape(*lengths[:dim], lengths[dim] * lengths[dim + 1], *lengths[dim + 2 :])


def exchange_both(x, axis, axes, splits, concats):
    sizes = [lax.axis_size(a) for a in axes]
    tiles = in_blocks(x, splits[0], sizes[0])
    tiles = jnp.moveaxis(in_blocks(tiles, splits[1] + 1, sizes[1]), 0, 1)
    inside = tiles.shape[2:]
    tiles = tiles.reshape(-1, *inside)
    tiles = lax.all_to_all(tiles, axis, split_axis=0, concat_axis=0, tiled=True)
    tiles = in_order(tiles.reshape(*sizes, *inside), concats[0] + 1)
    return in_order(tiles, concats[1])


def expert_slice(rows_in, expert_in, expert_out):
    width = rows_in.shape[1]
    slice_width = expert_in.shape[3]
    gate_up = jnp.dot(
        rows_in, expert_in[0].reshape(width, 2 * slice_width), preferred_element_type=jnp.float32
    )
    activated = (jax.nn.silu(gate_up[:, :slice_width]) * gate_up[:, slice_width:]).astype(
        jnp.bfloat16
    )
    return jnp.dot(activated, expert_out[0], preferred_element_type=jnp.float32).astype(
        jnp.bfloat16
    )


def shards(
    hidden_in,
    queries,
    latent_cache,
    lengths,
    w_uv,
    attn_weight,
    norm_gain,
    router,
    routes,
    live_counts,
    expert_in,
    expert_out,
):
    count_of_tokens, width = hidden_in.shape
    sections = lax.axis_size("sec")
    expert_groups = lax.axis_size(GRP)
    slices = lax.axis_size("tp")
    latent_width = w_uv.shape[2]
    query_block = queries[:, :, 0, :]
    scores = (
        jnp.einsum("bhr,bpr->bhp", query_block, latent_cache, preferred_element_type=jnp.float32)
        * score_scale
    )
    positions = jnp.arange(latent_cache.shape[1])
    visible = positions[None, None, :] < lengths[:, None, None]
    scores = jnp.where(visible, scores, -1e30)
    highest = jnp.max(scores, axis=2, keepdims=True)
    raised = jnp.exp(scores - highest)
    softmax_weights = (raised / jnp.sum(raised, axis=2, keepdims=True)).astype(jnp.bfloat16)
    latent_out = jnp.einsum(
        "bhp,bpc->bhc",
        softmax_weights,
        latent_cache[:, :, :latent_width],
        preferred_element_type=jnp.float32,
    ).astype(jnp.bfloat16)
    head_out = jnp.einsum(
        "bhc,hcv->bhv", latent_out, w_uv[:, 0], preferred_element_type=jnp.float32
    ).astype(jnp.bfloat16)
    head_rows = head_out.reshape(head_out.shape[0], -1)
    out_block = attn_weight[:, 0].reshape(-1, attn_weight.shape[3])
    partial_value = jnp.dot(
        gathered_by_axis(head_rows, GRP, 0), out_block, preferred_element_type=jnp.float32
    )
    partial_value = partial_value.reshape(
        expert_groups, slices, count_of_tokens, partial_value.shape[1]
    )
    summed = sent_and_summed(partial_value.astype(jnp.bfloat16), "tp", 1)
    column_part = summed[:, 0].astype(jnp.bfloat16)
    attention = lax.all_to_all(column_part, GRP, split_axis=0, concat_axis=2, tiled=True)[0]
    residual = hidden_in.astype(jnp.float32) + attention.astype(jnp.float32)
    normalized_input = (
        residual
        * lax.rsqrt(jnp.mean(residual * residual, axis=1, keepdims=True) + 1e-06)
        * norm_gain
    ).astype(jnp.bfloat16)
    experts = router.shape[1]
    per_token = routes.shape[1]
    capacity = max(2, 2 * count_of_tokens * per_token // experts)
    affinity = jax.nn.sigmoid(jnp.dot(normalized_input, router, preferred_element_type=jnp.float32))
    picked = routes[:, :, None] == jnp.arange(experts)[None, None, :]
    chosen = jnp.sum(jnp.where(picked, affinity[:, None, :], 0.0), axis=2)
    living = jnp.arange(count_of_tokens) < live_counts[0]
    gate_weights = (
        route_scale
        * chosen
        / jnp.sum(chosen, axis=1, keepdims=True)
        * living[:, None].astype(jnp.float32)
    )
    routed = jnp.any(picked, axis=1) & living[:, None]
    routed_count = routed.astype(jnp.int32)
    slot_index = jnp.cumsum(routed_count, axis=0) - routed_count
    placed_tokens = routed[:, :, None] & (
        slot_index[:, :, None] == jnp.arange(capacity)[None, None, :]
    )
    expert_gate = jnp.sum(jnp.where(picked, gate_weights[:, :, None], 0.0), axis=1)
    outgoing = jnp.einsum(
        "poy,pj->oyj",
        placed_tokens.astype(jnp.bfloat16),
        normalized_input,
        preferred_element_type=jnp.float32,
    ).astype(jnp.bfloat16)
    combine_rows = (placed_tokens.astype(jnp.float32) * expert_gate[:, :, None]).reshape(
        count_of_tokens, experts * capacity
    )
    once_rows = outgoing.reshape(sections, expert_groups, capacity, width)
    arrived = exchange_both(once_rows, SEC_GRP, ("sec", GRP), (0, 1), (0, 1))
    local_rows = arrived.reshape(-1, width)
    every_out = expert_slice(
        lax.all_gather(local_rows, "tp", axis=0, tiled=True), expert_in, expert_out
    )
    own_sums = lax.psum_scatter(
        every_out.astype(jnp.float32).astype(jnp.bfloat16), "tp", scatter_dimension=0, tiled=True
    ).astype(jnp.float32)
    own_sums = own_sums.reshape(sections, expert_groups, capacity, width)
    back_rows = exchange_both(
        own_sums.astype(jnp.bfloat16), GRP_SEC, (GRP, "sec"), (1, 0), (1, 0)
    ).astype(own_sums.dtype)
    expert_sums = back_rows.reshape(experts * capacity, width)
    expert_mix = jnp.dot(combine_rows, expert_sums, precision=lax.Precision.HIGHEST)
    return (residual + expert_mix).astype(jnp.bfloat16)


def solution(mesh):
    torus = Mesh(
        mesh.devices.reshape(mesh.shape["sec"], 8, 2, mesh.shape["tp"]),
        ("sec", "grp_0", "grp_1", "tp"),
    )
    in_specs = (
        P(SEC_GRP_TP, None),
        P(SEC_GRP, None, "tp", None),
        P(SEC_GRP, None, None),
        P(SEC_GRP),
        P(None, "tp", None, None),
        P(None, "tp", None, GRP),
        P(),
        P(),
        P(SEC_GRP_TP, None),
        P(SEC_GRP_TP),
        P(SEC_GRP, None, None, "tp"),
        P(SEC_GRP, "tp", None),
    )
    out_specs = P(SEC_GRP_TP, None)
    return jax.shard_map(
        shards, mesh=torus, in_specs=in_specs, out_specs=out_specs, check_vma=False
    )
```

profile of v0, /device:TPU:8, one launch (start us, length us, event | category | flops | bytes accessed | tf_op | source)
XLA Modules:
  0.0 292.9 jit_solution(1517495895846176154)
XLA Ops:
  6.5 0.9 iota_compare_fusion.1
  7.4 2.9 fusion.29
  10.3 0.2 fusion.52
  10.5 2.5 fusion.19
  13.1 0.6 fusion.33
  13.7 7.5 %all_gather.9 = bf16[64,2048]{1,0:T(8,128)(2,1)} all-gather(bf16[32,2048]{1,0:T(8,128)(2,1)S(1)} %bitcast.86), channel_id=1, replica_groups=mesh['sec'=2,'grp_0'=8,'grp_1'=2,'tp'=8] {'grp_1'}, dimensions={0}, use_global_device_ids=true | all-gather | bytes 393216 | tf_op jit(solution)/shard_map/all_gather | solution.py:18
  21.9 3.9 %copy.34 = bf16[16,1,128,448]{2,0,3,1:T(8,128)(2,1)} copy(bf16[16,1,128,448]{2,3,1,0:T(8,128)(2,1)} %param.17) | data formatting | bytes 3670016 | tf_op args[5]
  25.9 3.9 %reshape.224 = bf16[2048,448,1,1]{0,1,2,3:T(8,128)(2,1)} reshape(bf16[16,1,128,448]{2,0,3,1:T(8,128)(2,1)} %copy.34) | data formatting | bytes 3670016 | tf_op jit(solution)/shard_map/reshape;squeeze | solution.py:105
  29.7 35.4 %all-gather.3.cloned.1.call-done = bf16[512,2048]{1,0:T(8,128)(2,1)} async-done(((bf16[64,2048]{1,0:T(8,128)(2,1)}), bf16[512,2048]{1,0:T(8,128)(2,1)}) %all-gather.3.cloned.1.call-update) | async-done | bytes 2097168 | tf_op jit(solution)/shard_map/all_gather | solution.py:18
  65.2 4.1 %dot_general.32 = bf16[16,8,4,2048]{3,2,1,0:T(4,128)(2,1)} reshape(bf16[512,2048]{1,0:T(8,128)(2,1)} %all-gather.3.cloned.1.call-done) | data formatting | bytes 4194304 | tf_op jit(solution)/shard_map/dot_general | solution.py:106
  69.3 3.6 %fusion.22 = bf16[8,16,1,4,448]{4,0,3,1,2:T(8,128)(2,1)S(1)} fusion(bf16[2048,448,1,1]{0,1,2,3:T(8,128)(2,1)} %reshape.224, bf16[16,8,4,2048]{3,2,1,0:T(4,128)(2,1)} %dot_general.32), kind=kOutput, calls=%fused_computation.19 | convolution fusion | flops 939753472 | bytes 4390912 | tf_op jit(solution)/shard_map/dot_general | solution.py:106
  72.9 1.1 copy.36
  74.0 4.3 %all-to-all-start = ((bf16[8,16,1,4,448]{4,3,1,2,0:T(4,128)(2,1)}), bf16[8,16,1,4,448]{4,3,1,2,0:T(4,128)(2,1)S(1)}, u32[]{:S(2)}, u32[]{:S(2)}) async-start(bf16[8,16,1,4,448]{4,3,1,2,0:T(4,128)(2,1)} %copy.36), calls=%async_computation | async-start | bytes 1048576 | tf_op jit(solution)/shard_map/all_to_all | solution.py:30
  78.5 10.1 %all-to-all-done = bf16[8,16,1,4,448]{4,3,1,2,0:T(4,128)(2,1)S(1)} async-done(((bf16[8,16,1,4,448]{4,3,1,2,0:T(4,128)(2,1)}), bf16[8,16,1,4,448]{4,3,1,2,0:T(4,128)(2,1)S(1)}, u32[]{:S(2)}, u32[]{:S(2)}) %all-to-all-start) | async-done | bytes 458784 | tf_op jit(solution)/shard_map/all_to_all | solution.py:30
  88.5 0.9 reduce_sum.58
  89.4 5.9 %all-to-all-start.1 = ((bf16[16,4,448]{2,1,0:T(4,128)(2,1)}), bf16[16,4,448]{2,1,0:T(4,128)(2,1)S(1)}, u32[]{:S(2)}, u32[]{:S(2)}) async-start(bf16[16,4,448]{2,1,0:T(4,128)(2,1)} %reduce_sum.58), calls=%async_computation.1 | async-start | bytes 131072 | tf_op jit(solution)/shard_map/all_to_all | solution.py:114
  95.6 10.3 %all-to-all-done.1 = bf16[16,4,448]{2,1,0:T(4,128)(2,1)S(1)} async-done(((bf16[16,4,448]{2,1,0:T(4,128)(2,1)}), bf16[16,4,448]{2,1,0:T(4,128)(2,1)S(1)}, u32[]{:S(2)}, u32[]{:S(2)}) %all-to-all-start.1) | async-done | bytes 57376 | tf_op jit(solution)/shard_map/all_to_all | solution.py:114
  106.4 1.2 fusion.38
  108.2 0.4 fusion.1
  108.6 0.9 copy.43
  109.5 27.3 %all_to_all.24 = bf16[32,1,1,2,7168]{4,3,2,1,0:T(2,128)(2,1)S(1)} all-to-all(bf16[32,1,1,2,7168]{4,3,2,1,0:T(2,128)(2,1)S(1)} %copy.43), channel_id=1, replica_groups=mesh['sec'=2,'grp_0'=8,'grp_1'=2,'tp'=8] {'sec','grp_0','grp_1'}, dimensions={0} | all-to-all | bytes 1835008 | tf_op jit(solution)/shard_map/all_to_all | solution.py:46
  136.9 1.3 reshape_reshape.7
  138.4 43.3 %all-gather.5.cloned.1.call-done = bf16[512,7168]{1,0:T(8,128)(2,1)} async-done(((bf16[64,7168]{1,0:T(8,128)(2,1)}), bf16[512,7168]{1,0:T(8,128)(2,1)}) %all-gather.5.cloned.1.call-update) | async-done | bytes 7340048 | tf_op jit(solution)/shard_map/all_gather | solution.py:154
  181.7 6.3 %fusion.3 = f32[512,256]{1,0:T(8,128)S(1)} fusion(bf16[512,7168]{1,0:T(8,128)(2,1)} %all-gather.5.cloned.1.call-done, bf16[896,8,2,128]{3,2,1,0:T(2,128)(2,1)} %bitcast.88), kind=kOutput, calls=%fused_computation.6 | convolution fusion | flops 1879048192 | bytes 11534336 | tf_op jit(solution)/shard_map/dot_general | solution.py:54
  188.0 5.1 %convolution_convert_fusion = bf16[512,7168]{1,0:T(8,128)(2,1)} fusion(bf16[1,128,7168]{2,1,0:T(8,128)(2,1)S(1)} %copy-done.1, f32[512,256]{1,0:T(8,128)S(1)} %fusion.3), kind=kOutput, calls=%fused_computation.1 | convolution fusion | flops 943587328 | bytes 9699328 | tf_op jit(solution)/shard_map/dot_general | solution.py:60
  193.1 50.3 %reduce-scatter.2.cloned.1.call-done = bf16[64,7168]{1,0:T(8,128)(2,1)} async-done(((bf16[512,7168]{1,0:T(8,128)(2,1)}), bf16[64,7168]{1,0:T(8,128)(2,1)}) %reduce-scatter.2.cloned.1.call-update) | async-done | bytes 917520 | tf_op jit(solution)/shard_map/reduce_scatter | solution.py:156
  243.5 2.3 convert_element_type.99
  245.8 0.6 copy.44
  246.4 34.7 %all_to_all.25 = bf16[32,1,1,2,7168]{4,3,2,1,0:T(2,128)(2,1)S(1)} all-to-all(bf16[32,1,1,2,7168]{4,3,2,1,0:T(2,128)(2,1)S(1)} %bitcast.83), channel_id=1, replica_groups=mesh['sec'=2,'grp_0'=8,'grp_1'=2,'tp'=8] {'grp_0','grp_1','sec'}, dimensions={0} | all-to-all | bytes 1835008 | tf_op jit(solution)/shard_map/all_to_all | solution.py:46
  281.1 1.6 copy.67
  282.7 2.5 reshape.221
  285.2 1.2 fusion.2
  (35 shorter events, 1.7 us)
Async XLA Ops:
  6.5 6.6 %copy-start = (bf16[16,1,512,128]{3,2,1,0:T(8,128)(2,1)S(1)}, bf16[16,1,512,128]{3,2,1,0:T(8,128)(2,1)}, u32[]{:S(2)}) copy-start(bf16[16,1,512,128]{3,2,1,0:T(8,128)(2,1)} %param.16) | copy-start | bytes 6291460
  6.5 58.6 %all-gather.3.cloned.1.call-start = ((), (), s32[]{:S(2)}) async-start(), calls=%async_computation.5 | async-start | bytes 2359296 | tf_op jit(solution)/shard_map/all_gather | solution.py:18
  72.9 5.4 %copy-start.4 = (s32[4,8]{1,0:T(4,128)S(1)}, s32[4,8]{1,0:T(4,128)}, u32[]{:S(2)}) copy-start(s32[4,8]{1,0:T(4,128)} %param.20) | copy-start | bytes 388
  72.9 33.2 %copy-start.2 = (bf16[4,7168]{1,0:T(4,128)(2,1)S(1)}, bf16[4,7168]{1,0:T(4,128)(2,1)}, u32[]{:S(2)}) copy-start(bf16[4,7168]{1,0:T(4,128)(2,1)} %param.12) | copy-start | bytes 172036
  72.9 33.4 %copy-start.3 = (f32[7168]{0:T(1024)S(1)}, f32[7168]{0:T(1024)}, u32[]{:S(2)}) copy-start(f32[7168]{0:T(1024)} %param.18) | copy-start | bytes 86020
  74.0 14.6 %all-to-all-start = ((bf16[8,16,1,4,448]{4,3,1,2,0:T(4,128)(2,1)}), bf16[8,16,1,4,448]{4,3,1,2,0:T(4,128)(2,1)S(1)}, u32[]{:S(2)}, u32[]{:S(2)}) async-start(bf16[8,16,1,4,448]{4,3,1,2,0:T(4,128)(2,1)} %copy.36), calls=%async_computation | async-start | bytes 1048576 | tf_op jit(solution)/shard_map/all_to_all | solution.py:30
  89.4 16.5 %all-to-all-start.1 = ((bf16[16,4,448]{2,1,0:T(4,128)(2,1)}), bf16[16,4,448]{2,1,0:T(4,128)(2,1)S(1)}, u32[]{:S(2)}, u32[]{:S(2)}) async-start(bf16[16,4,448]{2,1,0:T(4,128)(2,1)} %reduce_sum.58), calls=%async_computation.1 | async-start | bytes 131072 | tf_op jit(solution)/shard_map/all_to_all | solution.py:114
  95.4 86.3 %all-gather.5.cloned.1.call-start = ((), (), s32[]{:S(2)}) async-start(), calls=%async_computation.6 | async-start | bytes 8257536 | tf_op jit(solution)/shard_map/all_gather | solution.py:154
  138.1 105.3 %reduce-scatter.2.cloned.1.call-start = ((), (), s32[]{:S(2)}) async-start(), calls=%async_computation.7 | async-start | bytes 8257536 | tf_op jit(solution)/shard_map/reduce_scatter | solution.py:156
  181.7 6.3 %copy-start.1 = (bf16[1,128,7168]{2,1,0:T(8,128)(2,1)S(1)}, bf16[1,128,7168]{2,1,0:T(8,128)(2,1)}, u32[]{:S(2)}) copy-start(bf16[1,128,7168]{2,1,0:T(8,128)(2,1)} %param.23) | copy-start | bytes 5505028
Sparse Core Ops, SparseCore 0:
  21.4 43.7 all-gather.2
  138.3 43.3 all-gather.4
  193.2 50.1 reduce-scatter.1
where the time goes:
time: 294 us; the launch traced here: 293 us
  waiting for transfers between devices  150 us (51%)
  blocking collectives  69.6 us (24%)
  matrix products  23.8 us (8%)
  local copies, waits for them, and re-layouts  22.7 us (8%)
  between operations  14 us (5%)
  starting transfers between devices  10.5 us (4%)
    all_to_all x2, blocking collectives, exchange_both(): tiles = lax.all_to_all(tiles, axis, split_axis=0, concat_axis=0, tiled=True)  62 us
    reduce_scatter x1, waiting for transfers between devices, shards(): lax.psum_scatter(every_out.astype(jnp.float32).astype(jnp.bfloat16), 'tp'...  50.3 us
    all_gather x1, waiting for transfers between devices, shards(): lax.all_gather(local_rows, 'tp', axis=0, tiled=True)  43.3 us
    all_gather x1, waiting for transfers between devices, gathered_by_axis(): out = lax.all_gather(out, axes[number], axis=dim, tiled=True)  35.4 us
    all_to_all x1, waiting for transfers between devices, shards(): lax.all_to_all(column_part, GRP, split_axis=0, concat_axis=2, tiled=True)[0]  10.3 us
    all_to_all x1, waiting for transfers between devices, sent_and_summed(): lax.all_to_all(tiles, axis, split_axis=0, concat_axis=0, tiled=True)  10.1 us
    all_gather x1, blocking collectives, gathered_by_axis(): out = lax.all_gather(out, axes[number], axis=dim, tiled=True)  7.51 us
    dot_general x1, matrix products, expert_slice(): jnp.dot(rows_in, expert_in[0].reshape(width, 2 * slice_width), preferred_...  6.32 us
  transfers between devices with their start and end apart: 5, of which 5 were waited for; matrix products, arithmetic and copies ran while one was open for 3% of the time, Pallas kernels for 0%

commit v1 on v0

--- a/solution.py
+++ b/solution.py
@@ -151,7 +151,11 @@
     arrived = exchange_both(once_rows, SEC_GRP, ("sec", GRP), (0, 1), (0, 1))
     local_rows = arrived.reshape(-1, width)
     every_out = expert_slice(
-        lax.all_gather(local_rows, "tp", axis=0, tiled=True), expert_in, expert_out
+        jnp.concatenate(
+            lax.all_to_all(jnp.stack([local_rows] * lax.axis_size("tp")), "tp", 0, 0), axis=0
+        ),
+        expert_in,
+        expert_out,
     )
     own_sums = lax.psum_scatter(
         every_out.astype(jnp.float32).astype(jnp.bfloat16), "tp", scatter_dimension=0, tiled=True

time: 294 us -> 330 us (1.12)
  blocking collectives: 69.6 us -> 156 us
  waiting for transfers between devices: 150 us -> 102 us
  matrix products: 23.8 us -> 19.6 us
    all_to_all x0 -> x1, blocking collectives: none -> 86.2 us  [shards(): lax.all_to_all(jnp.stack([local_rows] * lax.axis_size('tp')), 'tp', 0, 0)]
    all_gather x1 -> x0, waiting for transfers between devices: 43.3 us -> none  [shards(): lax.all_gather(local_rows, 'tp', axis=0, tiled=True)]
    dot_general x1, matrix products: 6.32 us -> 2.14 us  [expert_slice(): jnp.dot(rows_in, expert_in[0].reshape(width, 2 * slice_width), preferred_...]
    reduce_scatter x1, waiting for transfers between devices: 50.3 us -> 46.2 us  [shards(): lax.psum_scatter(every_out.astype(jnp.float32).astype(jnp.bfloat16), 'tp'...]
  transfers between devices with their start and end apart: 5 -> 4, of which waited for: 5 -> 4; matrix products, arithmetic and copies ran while one was open for 3% -> 2% of each run, Pallas kernels for 0% -> 0%
where the time goes in v1:
time: 330 us
  blocking collectives  156 us (47%)
  waiting for transfers between devices  102 us (31%)
  local copies, waits for them, and re-layouts  24.8 us (8%)
  matrix products  19.6 us (6%)
  between operations  14.3 us (4%)
  starting transfers between devices  10.2 us (3%)
    all_to_all x1, blocking collectives, shards(): lax.all_to_all(jnp.stack([local_rows] * lax.axis_size('tp')), 'tp', 0, 0)  86.2 us
    all_to_all x2, blocking collectives, exchange_both(): tiles = lax.all_to_all(tiles, axis, split_axis=0, concat_axis=0, tiled=True)  62 us
    reduce_scatter x1, waiting for transfers between devices, shards(): lax.psum_scatter(every_out.astype(jnp.float32).astype(jnp.bfloat16), 'tp'...  46.2 us
    all_gather x1, waiting for transfers between devices, gathered_by_axis(): out = lax.all_gather(out, axes[number], axis=dim, tiled=True)  35.4 us
    all_to_all x1, waiting for transfers between devices, shards(): lax.all_to_all(column_part, GRP, split_axis=0, concat_axis=2, tiled=True)[0]  10.3 us
    all_to_all x1, waiting for transfers between devices, sent_and_summed(): lax.all_to_all(tiles, axis, split_axis=0, concat_axis=0, tiled=True)  10.1 us
    all_gather x1, blocking collectives, gathered_by_axis(): out = lax.all_gather(out, axes[number], axis=dim, tiled=True)  7.51 us
  transfers between devices with their start and end apart: 4, of which 4 were waited for; matrix products, arithmetic and copies ran while one was open for 2% of the time, Pallas kernels for 0%

profile of v1, /device:TPU:8, one launch (start us, length us, event | category | flops | bytes accessed | tf_op | source)
XLA Modules:
  0.0 329.5 jit_solution(11342503244446615319)
XLA Ops:
  6.5 0.9 iota_compare_fusion.1
  7.4 2.9 fusion.29
  10.5 2.5 fusion.19
  13.1 0.6 fusion.33
  13.7 7.5 %all_gather.6 = bf16[64,2048]{1,0:T(8,128)(2,1)} all-gather(bf16[32,2048]{1,0:T(8,128)(2,1)S(1)} %bitcast.88), channel_id=1, replica_groups=mesh['sec'=2,'grp_0'=8,'grp_1'=2,'tp'=8] {'grp_1'}, dimensions={0}, use_global_device_ids=true | all-gather | bytes 393216 | tf_op jit(solution)/shard_map/all_gather | solution.py:18
  21.9 3.9 %copy.34 = bf16[16,1,128,448]{2,0,3,1:T(8,128)(2,1)} copy(bf16[16,1,128,448]{2,3,1,0:T(8,128)(2,1)} %param.17) | data formatting | bytes 3670016 | tf_op args[5]
  25.9 3.9 %reshape.230 = bf16[2048,448,1,1]{0,1,2,3:T(8,128)(2,1)} reshape(bf16[16,1,128,448]{2,0,3,1:T(8,128)(2,1)} %copy.34) | data formatting | bytes 3670016 | tf_op jit(solution)/shard_map/reshape;squeeze | solution.py:105
  29.7 35.4 %all-gather.2.cloned.1.call-done = bf16[512,2048]{1,0:T(8,128)(2,1)} async-done(((bf16[64,2048]{1,0:T(8,128)(2,1)}), bf16[512,2048]{1,0:T(8,128)(2,1)}) %all-gather.2.cloned.1.call-update) | async-done | bytes 2097168 | tf_op jit(solution)/shard_map/all_gather | solution.py:18
  65.2 4.1 %dot_general.32 = bf16[16,8,4,2048]{3,2,1,0:T(4,128)(2,1)} reshape(bf16[512,2048]{1,0:T(8,128)(2,1)} %all-gather.2.cloned.1.call-done) | data formatting | bytes 4194304 | tf_op jit(solution)/shard_map/dot_general | solution.py:106
  69.3 3.6 %fusion.22 = bf16[8,16,1,4,448]{4,0,3,1,2:T(8,128)(2,1)S(1)} fusion(bf16[2048,448,1,1]{0,1,2,3:T(8,128)(2,1)} %reshape.230, bf16[16,8,4,2048]{3,2,1,0:T(4,128)(2,1)} %dot_general.32), kind=kOutput, calls=%fused_computation.19 | convolution fusion | flops 939753472 | bytes 4390912 | tf_op jit(solution)/shard_map/dot_general | solution.py:106
  72.9 1.1 copy.36
  74.0 4.3 %all-to-all-start = ((bf16[8,16,1,4,448]{4,3,1,2,0:T(4,128)(2,1)}), bf16[8,16,1,4,448]{4,3,1,2,0:T(4,128)(2,1)S(1)}, u32[]{:S(2)}, u32[]{:S(2)}) async-start(bf16[8,16,1,4,448]{4,3,1,2,0:T(4,128)(2,1)} %copy.36), calls=%async_computation | async-start | bytes 1048576 | tf_op jit(solution)/shard_map/all_to_all | solution.py:30
  78.5 10.1 %all-to-all-done = bf16[8,16,1,4,448]{4,3,1,2,0:T(4,128)(2,1)S(1)} async-done(((bf16[8,16,1,4,448]{4,3,1,2,0:T(4,128)(2,1)}), bf16[8,16,1,4,448]{4,3,1,2,0:T(4,128)(2,1)S(1)}, u32[]{:S(2)}, u32[]{:S(2)}) %all-to-all-start) | async-done | bytes 458784 | tf_op jit(solution)/shard_map/all_to_all | solution.py:30
  88.5 0.9 reduce_sum.58
  89.4 5.9 %all-to-all-start.1 = ((bf16[16,4,448]{2,1,0:T(4,128)(2,1)}), bf16[16,4,448]{2,1,0:T(4,128)(2,1)S(1)}, u32[]{:S(2)}, u32[]{:S(2)}) async-start(bf16[16,4,448]{2,1,0:T(4,128)(2,1)} %reduce_sum.58), calls=%async_computation.1 | async-start | bytes 131072 | tf_op jit(solution)/shard_map/all_to_all | solution.py:114
  95.6 10.3 %all-to-all-done.1 = bf16[16,4,448]{2,1,0:T(4,128)(2,1)S(1)} async-done(((bf16[16,4,448]{2,1,0:T(4,128)(2,1)}), bf16[16,4,448]{2,1,0:T(4,128)(2,1)S(1)}, u32[]{:S(2)}, u32[]{:S(2)}) %all-to-all-start.1) | async-done | bytes 57376 | tf_op jit(solution)/shard_map/all_to_all | solution.py:114
  106.4 1.2 fusion.38
  108.2 0.4 fusion.1
  108.6 0.9 copy.43
  109.5 27.3 %all_to_all.29 = bf16[32,1,1,2,7168]{4,3,2,1,0:T(2,128)(2,1)S(1)} all-to-all(bf16[32,1,1,2,7168]{4,3,2,1,0:T(2,128)(2,1)S(1)} %copy.43), channel_id=1, replica_groups=mesh['sec'=2,'grp_0'=8,'grp_1'=2,'tp'=8] {'sec','grp_0','grp_1'}, dimensions={0} | all-to-all | bytes 1835008 | tf_op jit(solution)/shard_map/all_to_all | solution.py:46
  136.9 1.3 stack_reshape_reshape.2
  138.1 2.1 stack.3
  140.2 86.2 %all_to_all.30 = bf16[8,64,7168]{2,1,0:T(8,128)(2,1)S(1)} all-to-all(bf16[8,64,7168]{2,1,0:T(8,128)(2,1)S(1)} %stack.3), channel_id=1, replica_groups=mesh['sec'=2,'grp_0'=8,'grp_1'=2,'tp'=8] {'tp'}, dimensions={0} | all-to-all | bytes 14680064 | tf_op jit(solution)/shard_map/all_to_all | solution.py:155
  226.4 2.1 fusion.3
  228.6 5.1 %convolution_convert_fusion = bf16[512,7168]{1,0:T(8,128)(2,1)} fusion(bf16[1,128,7168]{2,1,0:T(8,128)(2,1)S(1)} %copy-done.1, f32[512,256]{1,0:T(8,128)S(1)} %fusion.3), kind=kOutput, calls=%fused_computation.1 | convolution fusion | flops 943587328 | bytes 9699328 | tf_op jit(solution)/shard_map/dot_general | solution.py:60
  233.6 46.2 %reduce-scatter.2.cloned.1.call-done = bf16[64,7168]{1,0:T(8,128)(2,1)} async-done(((bf16[512,7168]{1,0:T(8,128)(2,1)}), bf16[64,7168]{1,0:T(8,128)(2,1)}) %reduce-scatter.2.cloned.1.call-update) | async-done | bytes 917520 | tf_op jit(solution)/shard_map/reduce_scatter | solution.py:160
  279.8 2.3 convert_element_type.99
  282.2 0.6 copy.44
  282.8 34.7 %all_to_all.31 = bf16[32,1,1,2,7168]{4,3,2,1,0:T(2,128)(2,1)S(1)} all-to-all(bf16[32,1,1,2,7168]{4,3,2,1,0:T(2,128)(2,1)S(1)} %bitcast.85), channel_id=1, replica_groups=mesh['sec'=2,'grp_0'=8,'grp_1'=2,'tp'=8] {'grp_0','grp_1','sec'}, dimensions={0} | all-to-all | bytes 1835008 | tf_op jit(solution)/shard_map/all_to_all | solution.py:46
  317.5 1.6 copy.67
  319.0 2.5 reshape.227
  321.5 1.2 fusion.2
  (36 shorter events, 1.7 us)
Async XLA Ops:
  6.5 6.6 %copy-start = (bf16[16,1,512,128]{3,2,1,0:T(8,128)(2,1)S(1)}, bf16[16,1,512,128]{3,2,1,0:T(8,128)(2,1)}, u32[]{:S(2)}) copy-start(bf16[16,1,512,128]{3,2,1,0:T(8,128)(2,1)} %param.16) | copy-start | bytes 6291460
  6.5 58.6 %all-gather.2.cloned.1.call-start = ((), (), s32[]{:S(2)}) async-start(), calls=%async_computation.6 | async-start | bytes 2359296 | tf_op jit(solution)/shard_map/all_gather | solution.py:18
  72.9 5.4 %copy-start.4 = (s32[4,8]{1,0:T(4,128)S(1)}, s32[4,8]{1,0:T(4,128)}, u32[]{:S(2)}) copy-start(s32[4,8]{1,0:T(4,128)} %param.20) | copy-start | bytes 388
  72.9 33.2 %copy-start.2 = (bf16[4,7168]{1,0:T(4,128)(2,1)S(1)}, bf16[4,7168]{1,0:T(4,128)(2,1)}, u32[]{:S(2)}) copy-start(bf16[4,7168]{1,0:T(4,128)(2,1)} %param.12) | copy-start | bytes 172036
  72.9 33.4 %copy-start.3 = (f32[7168]{0:T(1024)S(1)}, f32[7168]{0:T(1024)}, u32[]{:S(2)}) copy-start(f32[7168]{0:T(1024)} %param.18) | copy-start | bytes 86020
  74.0 14.6 %all-to-all-start = ((bf16[8,16,1,4,448]{4,3,1,2,0:T(4,128)(2,1)}), bf16[8,16,1,4,448]{4,3,1,2,0:T(4,128)(2,1)S(1)}, u32[]{:S(2)}, u32[]{:S(2)}) async-start(bf16[8,16,1,4,448]{4,3,1,2,0:T(4,128)(2,1)} %copy.36), calls=%async_computation | async-start | bytes 1048576 | tf_op jit(solution)/shard_map/all_to_all | solution.py:30
  89.4 16.5 %all-to-all-start.1 = ((bf16[16,4,448]{2,1,0:T(4,128)(2,1)}), bf16[16,4,448]{2,1,0:T(4,128)(2,1)S(1)}, u32[]{:S(2)}, u32[]{:S(2)}) async-start(bf16[16,4,448]{2,1,0:T(4,128)(2,1)} %reduce_sum.58), calls=%async_computation.1 | async-start | bytes 131072 | tf_op jit(solution)/shard_map/all_to_all | solution.py:114
  95.4 184.4 %reduce-scatter.2.cloned.1.call-start = ((), (), s32[]{:S(2)}) async-start(), calls=%async_computation.7 | async-start | bytes 8257536 | tf_op jit(solution)/shard_map/reduce_scatter | solution.py:160
  140.2 86.2 %copy-start.5 = (bf16[1,7168,2,128]{3,2,1,0:T(2,128)(2,1)S(1)}, bf16[1,7168,2,128]{3,2,1,0:T(2,128)(2,1)}, u32[]{:S(2)}) copy-start(bf16[1,7168,2,128]{3,2,1,0:T(2,128)(2,1)} %param.22) | copy-start | bytes 11010052
  226.4 2.2 copy-start.1
Sparse Core Ops, SparseCore 0:
  21.4 43.7 all-gather.1
  233.8 45.9 reduce-scatter.1
